TPU v7x, 32 devices: a whole 2x2x4 slice. The times are simulated.
32 devices in a mesh: dp: 2 (over x), context: 4 (over z), tensor: 4 (over y, core).
Axes of the slice: x: 2, y: 2, z: 4, core: 2. Of those that a mesh axis runs over, the one named last changes fastest.
Arguments:
- tokens: bfloat16 [6144, 640], P(('dp', 'context')), may hold values from -8 to 8
- seq_lengths: int32 [2, 2], P('dp'), may hold values from 1 to 2048, 3072 in all within a row
- input_gain: bfloat16 [640], P('dp'), may hold values from 0.25 to 1.75
- query_weight: bfloat16 [640, 1024], P('dp', 'tensor'), may hold values from -0.25 to 0.25
- key_weight: bfloat16 [640, 256], P('dp'), may hold values from -0.25 to 0.25
- value_weight: bfloat16 [640, 256], P('dp'), may hold values from -0.25 to 0.25
- query_gain: bfloat16 [256], P('dp'), may hold values from 0.25 to 1.75
- key_gain: bfloat16 [256], P('dp'), may hold values from 0.25 to 1.75
- output_weight: bfloat16 [1024, 640], P('tensor', 'dp'), may hold values from -0.1875 to 0.1875
- attention_gain: bfloat16 [640], P('dp'), may hold values from 0.25 to 1.75
- prefeed_gain: bfloat16 [640], P('dp'), may hold values from 0.25 to 1.75
- gate_weight: bfloat16 [640, 2048], P('dp', 'tensor'), may hold values from -0.25 to 0.25
- up_weight: bfloat16 [640, 2048], P('dp', 'tensor'), may hold values from -0.25 to 0.25
- down_weight: bfloat16 [2048, 640], P('tensor', 'dp'), may hold values from -0.125 to 0.125
- feed_gain: bfloat16 [640], P('dp'), may hold values from 0.25 to 1.75
- cotangent: bfloat16 [6144, 640], P(('dp', 'context')), may hold values from -8 to 8
Outputs:
- layer_out: bfloat16 [6144, 640], P(('dp', 'context'))
- tokens_grad: float32 [6144, 640], P(('dp', 'context'))
- input_gain_grad: float32 [640], P('dp')
- query_weight_grad: float32 [640, 1024], P('dp', 'tensor')
- key_weight_grad: float32 [640, 256], P('dp')
- value_weight_grad: float32 [640, 256], P('dp')
- query_gain_grad: float32 [256], P('dp')
- key_gain_grad: float32 [256], P('dp')
- output_weight_grad: float32 [1024, 640], P('tensor', 'dp')
- attention_gain_grad: float32 [640], P('dp')
- prefeed_gain_grad: float32 [640], P('dp')
- gate_weight_grad: float32 [640, 2048], P('dp', 'tensor')
- up_weight_grad: float32 [640, 2048], P('dp', 'tensor')
- down_weight_grad: float32 [2048, 640], P('tensor', 'dp')
- feed_gain_grad: float32 [640], P('dp')
Inputs may be any that keep to these rules, and one draw needn't show every extreme that they name: `seq_lengths`: each row lists 2 lengths that add up to 3072, none above 2048.
All inputs are finite; a program needn't handle non-finite values.
Results may differ from a plain program's by a relative error of at most 0.022.
Values may be sent and summed in bfloat16 or wider, within the bound.
No kernel may reach another device: no remote copies, remote signals or barrier semaphores. Data moves between devices by JAX's collectives and lax.ppermute only.
A program may use at most 128 MiB of HBM per device.

v0:
```python
import math
import jax
import jax.numpy as jnp
from jax import lax
from jax.sharding import PartitionSpec as P

HD = 256
LMAX = 2048
EPS = 1e-06
NEG = -1000000000.0
SCALE = 0.0625


def passed_along(array, axis, by):
    devices = lax.axis_size(axis)
    pairs = [(i, i + by) for i in range(devices) if 0 <= i + by < devices]
    return lax.ppermute(array, axis, pairs)


def shortened(array):

    def short(part):
        return part.astype(jnp.bfloat16) if part.dtype == jnp.float32 else part

    return jax.tree.map(short, array)


def product(left_side, right_side):
    return jnp.dot(left_side, right_side, preferred_element_type=jnp.float32)


def product_lt(left_side, right_side):
    return lax.dot_general(
        left_side, right_side, (((0,), (0,)), ((), ())), preferred_element_type=jnp.float32
    )


def product_rt(left_side, right_side):
    return lax.dot_general(
        left_side, right_side, (((1,), (1,)), ((), ())), preferred_element_type=jnp.float32
    )


def rms_norm(values, scale_gain):
    return values * lax.rsqrt(jnp.mean(values * values, axis=-1, keepdims=True) + EPS) * scale_gain


def rotate(values, position):
    half_width = values.shape[-1] // 2
    frequency = jnp.exp(
        jnp.arange(half_width, dtype=jnp.float32) * (-2.0 * math.log(1000000.0) / values.shape[-1])
    )
    angles = position.astype(jnp.float32).reshape((-1,) + (1,) * (values.ndim - 1)) * frequency
    cosines = jnp.cos(angles)
    sines = jnp.sin(angles)
    first_half = values[..., :half_width]
    second_half = values[..., half_width:]
    return jnp.concatenate(
        [first_half * cosines - second_half * sines, second_half * cosines + first_half * sines],
        axis=-1,
    )


def layout(lengths, row_index):
    seq_ends = jnp.cumsum(lengths)
    starts = seq_ends - lengths
    member = (
        (row_index[:, None] >= starts[None, :]) & (row_index[:, None] < seq_ends[None, :])
    ).astype(jnp.int32)
    number = jnp.arange(lengths.shape[0], dtype=jnp.int32)
    segment = jnp.sum(member * (number[None, :] + 1), axis=1) - 1
    position = row_index - jnp.sum(member * starts[None, :], axis=1)
    return (segment, position)


def block_scores(query, key_block, allowed):
    scores = jnp.einsum("qhd,kd->hqk", query, key_block, preferred_element_type=jnp.float32) * SCALE
    return jnp.where(allowed[None], scores, NEG)


def local(
    tokens,
    seq_lengths,
    input_gain,
    query_weight,
    key_weight,
    value_weight,
    query_gain,
    key_gain,
    output_weight,
    attention_gain,
    prefeed_gain,
    gate_weight,
    up_weight,
    down_weight,
    feed_gain,
    cotangent,
):
    row_count = tokens.shape[0]
    chain_width = lax.axis_size("context")
    chain_place = lax.axis_index("context")
    chain_reach = min(chain_width - 1, (LMAX - 2) // row_count + 1)
    lengths = seq_lengths[0]
    own_index = chain_place * row_count + jnp.arange(row_count, dtype=jnp.int32)
    own_segment, own_position = layout(lengths, own_index)
    w_query, w_key, w_value, w_output, g_input, g_attention, g_query, g_key = (
        lax.all_gather(query_weight, "dp", axis=0, tiled=True),
        lax.all_gather(key_weight, "dp", axis=0, tiled=True),
        lax.all_gather(value_weight, "dp", axis=0, tiled=True),
        lax.all_gather(output_weight, "dp", axis=1, tiled=True),
        lax.all_gather(input_gain, "dp", axis=0, tiled=True),
        lax.all_gather(attention_gain, "dp", axis=0, tiled=True),
        lax.all_gather(query_gain, "dp", axis=0, tiled=True),
        lax.all_gather(key_gain, "dp", axis=0, tiled=True),
    )
    w_gate, w_up, w_down, g_prefeed, g_feed = (
        lax.all_gather(gate_weight, "dp", axis=0, tiled=True),
        lax.all_gather(up_weight, "dp", axis=0, tiled=True),
        lax.all_gather(down_weight, "dp", axis=1, tiled=True),
        lax.all_gather(prefeed_gain, "dp", axis=0, tiled=True),
        lax.all_gather(feed_gain, "dp", axis=0, tiled=True),
    )
    g_input = g_input.astype(jnp.float32)
    g_attention = g_attention.astype(jnp.float32)
    g_query = g_query.astype(jnp.float32)
    g_key = g_key.astype(jnp.float32)
    g_prefeed = g_prefeed.astype(jnp.float32)
    g_feed = g_feed.astype(jnp.float32)
    local_heads = w_query.shape[1] // HD
    stream = tokens.astype(jnp.float32)
    normed_full, input_back = jax.vjp(rms_norm, stream, g_input)
    normed = normed_full.astype(jnp.bfloat16)
    query_raw = product(normed, w_query).reshape(row_count, local_heads, HD)
    key_raw = product(normed, w_key)
    value = product(normed, w_value).astype(jnp.bfloat16)
    query_full, query_back = jax.vjp(
        lambda raw_part, gain_part: rotate(rms_norm(raw_part, gain_part), own_position),
        query_raw,
        g_query,
    )
    key_full, key_back = jax.vjp(
        lambda raw_part, gain_part: rotate(rms_norm(raw_part, gain_part), own_position),
        key_raw,
        g_key,
    )
    query = query_full.astype(jnp.bfloat16)
    key_rot = key_full.astype(jnp.bfloat16)
    blocks = []
    current = (key_rot, value)
    for step in range(chain_reach + 1):
        if step > 0:
            current = passed_along((current[0], current[1]), "context", 1)
        block_index = own_index - step * row_count
        block_segment = layout(lengths, block_index)[0]
        allowed = (own_segment[:, None] == block_segment[None, :]) & (
            block_index[None, :] <= own_index[:, None]
        )
        is_live = own_segment[0] == block_segment[row_count - 1]
        blocks.append((current[0], current[1], allowed, is_live))
    score_shape = (local_heads, row_count, row_count)
    kept_scores = []
    running_max = None
    total_mass = None
    for step in range(chain_reach + 1):
        key_block, value_block, allowed, is_live = blocks[step]

        def compute_block(key_block=key_block, allowed=allowed):
            scores = block_scores(query, key_block, allowed)
            peak = jnp.max(scores, axis=-1)
            return (scores, peak, jnp.sum(jnp.exp(scores - peak[..., None]), axis=-1))

        if step == 0:
            scores, peak, mass = compute_block()
            running_max, total_mass = (peak, mass)
        else:
            scores, peak, mass = compute_block()
            new_max = jnp.maximum(running_max, peak)
            total_mass = total_mass * jnp.exp(running_max - new_max) + mass * jnp.exp(
                peak - new_max
            )
            running_max = new_max
        kept_scores.append(scores)
    log_mass = running_max + jnp.log(total_mass)
    heads_out = jnp.zeros((row_count, local_heads, HD), jnp.float32)
    for step in range(chain_reach + 1):
        key_block, value_block, allowed, is_live = blocks[step]

        def compute_block(value_block=value_block, scores=kept_scores[step]):
            attn_probs = jnp.exp(scores - log_mass[..., None]).astype(jnp.bfloat16)
            return jnp.einsum(
                "hqk,kd->qhd", attn_probs, value_block, preferred_element_type=jnp.float32
            )

        if step == 0:
            heads_out = compute_block()
        else:
            heads_out = heads_out + compute_block()
    heads_low = heads_out.astype(jnp.bfloat16).reshape(row_count, local_heads * HD)
    attn_sum = lax.psum(product(heads_low, w_output).astype(jnp.bfloat16), "tensor").astype(
        jnp.float32
    )
    attn_post, attn_back = jax.vjp(rms_norm, attn_sum, g_attention)
    middle = stream + attn_post
    normed_feed_full, prefeed_back = jax.vjp(rms_norm, middle, g_prefeed)
    normed_feed = normed_feed_full.astype(jnp.bfloat16)
    gate_proj = product(normed_feed, w_gate)
    up_proj = product(normed_feed, w_up)
    activation, activation_back = jax.vjp(
        lambda gate_part, up_part: jax.nn.gelu(gate_part, approximate=True) * up_part,
        gate_proj,
        up_proj,
    )
    hidden = activation.astype(jnp.bfloat16)
    feed_sum = lax.psum(product(hidden, w_down).astype(jnp.bfloat16), "tensor").astype(jnp.float32)
    feed_post, feed_back = jax.vjp(rms_norm, feed_sum, g_feed)
    result = middle + feed_post
    layer_out = result.astype(jnp.bfloat16)
    grad_out = cotangent.astype(jnp.float32)
    grad_feed_full, grad_gfeed = feed_back(grad_out)
    grad_feed = grad_feed_full.astype(jnp.bfloat16)
    grad_wdown = product_lt(hidden, grad_feed)
    grad_hidden = product_rt(grad_feed, w_down)
    grad_gate_full, grad_up_full = activation_back(grad_hidden)
    grad_gate = grad_gate_full.astype(jnp.bfloat16)
    grad_up = grad_up_full.astype(jnp.bfloat16)
    grad_wgate = product_lt(normed_feed, grad_gate)
    grad_wup = product_lt(normed_feed, grad_up)
    grad_normed_feed = lax.psum(
        (product_rt(grad_gate, w_gate) + product_rt(grad_up, w_up)).astype(jnp.bfloat16), "tensor"
    ).astype(jnp.float32)
    grad_middle_norm, grad_gprefeed = prefeed_back(grad_normed_feed)
    grad_middle = grad_out + grad_middle_norm
    grad_attn_full, grad_gattention = attn_back(grad_middle)
    grad_attn = grad_attn_full.astype(jnp.bfloat16)
    grad_woutput = product_lt(heads_low, grad_attn)
    grad_heads = (
        product_rt(grad_attn, w_output).reshape(row_count, local_heads, HD).astype(jnp.bfloat16)
    )
    kept_blocks = []
    row_dots = jnp.zeros(score_shape[:2], jnp.float32)
    for step in range(chain_reach + 1):
        key_block, value_block, allowed, is_live = blocks[step]

        def compute_block(key_block=key_block, value_block=value_block, allowed=allowed):
            scores = block_scores(query, key_block, allowed)
            attn_probs = jnp.exp(scores - log_mass[..., None])
            prob_grad = jnp.einsum(
                "qhd,kd->hqk", grad_heads, value_block, preferred_element_type=jnp.float32
            )
            return (attn_probs, prob_grad, jnp.sum(attn_probs * prob_grad, axis=-1))

        if step == 0:
            attn_probs, prob_grad, partial_dots = compute_block()
        else:
            attn_probs, prob_grad, partial_dots = compute_block()
        row_dots = row_dots + partial_dots
        kept_blocks.append((attn_probs, prob_grad))
    grad_query = jnp.zeros((row_count, local_heads, HD), jnp.float32)
    carried = (jnp.zeros((row_count, HD), jnp.float32), jnp.zeros((row_count, HD), jnp.float32))
    for step in range(chain_reach, -1, -1):
        key_block, value_block, allowed, is_live = blocks[step]
        attn_probs, prob_grad = kept_blocks[step]

        def compute_block(key_block=key_block, attn_probs=attn_probs, prob_grad=prob_grad):
            grad_scores = (attn_probs * (prob_grad - row_dots[..., None])).astype(jnp.bfloat16)
            probs_low = attn_probs.astype(jnp.bfloat16)
            query_part = (
                jnp.einsum(
                    "hqk,kd->qhd", grad_scores, key_block, preferred_element_type=jnp.float32
                )
                * SCALE
            )
            key_part = (
                jnp.einsum("hqk,qhd->kd", grad_scores, query, preferred_element_type=jnp.float32)
                * SCALE
            )
            value_part = jnp.einsum(
                "hqk,qhd->kd", probs_low, grad_heads, preferred_element_type=jnp.float32
            )
            return (query_part, key_part, value_part)

        if step == 0:
            query_part, key_part, value_part = compute_block()
        else:
            query_part, key_part, value_part = compute_block()
        grad_query = grad_query + query_part
        carried = (carried[0] + key_part, carried[1] + value_part)
        if step > 0:
            carried = passed_along((shortened(carried[0]), shortened(carried[1])), "context", -1)
    grad_key, grad_value = (
        lax.psum(carried[0].astype(jnp.bfloat16), "tensor").astype(jnp.float32),
        lax.psum(carried[1].astype(jnp.bfloat16), "tensor").astype(jnp.float32),
    )
    grad_query_full, grad_gquery_part = query_back(grad_query)
    grad_key_full, grad_gkey = key_back(grad_key)
    grad_query_raw = grad_query_full.reshape(row_count, local_heads * HD).astype(jnp.bfloat16)
    grad_key_raw = grad_key_full.astype(jnp.bfloat16)
    grad_value_low = grad_value.astype(jnp.bfloat16)
    grad_wquery = product_lt(normed, grad_query_raw)
    grad_wkey = product_lt(normed, grad_key_raw)
    grad_wvalue = product_lt(normed, grad_value_low)
    grad_normed_part = product_rt(grad_query_raw, w_query)
    grad_normed_sum, grad_gquery = (
        lax.psum(grad_normed_part.astype(jnp.bfloat16), "tensor").astype(jnp.float32),
        lax.psum(grad_gquery_part.astype(jnp.bfloat16), "tensor").astype(jnp.float32),
    )
    grad_normed = (
        grad_normed_sum + product_rt(grad_key_raw, w_key) + product_rt(grad_value_low, w_value)
    )
    grad_stream_norm, grad_ginput = input_back(grad_normed)
    tokens_grad = grad_middle + grad_stream_norm
    totals = lax.psum(
        (
            grad_ginput,
            grad_wquery,
            grad_wkey,
            grad_wvalue,
            grad_gquery,
            grad_gkey,
            grad_woutput,
            grad_gattention,
            grad_gprefeed,
            grad_wgate,
            grad_wup,
            grad_wdown,
            grad_gfeed,
        ),
        ("dp", "context"),
    )
    shard_place = lax.axis_index("dp")
    shard_count = lax.axis_size("dp")
    slice_dims = (0, 0, 0, 0, 0, 0, 1, 0, 0, 0, 0, 1, 0)
    shares = tuple(
        (
            lax.dynamic_slice_in_dim(
                total_grad,
                shard_place * (total_grad.shape[dim_index] // shard_count),
                total_grad.shape[dim_index] // shard_count,
                dim_index,
            )
            for total_grad, dim_index in zip(totals, slice_dims)
        )
    )
    return (
        layer_out,
        tokens_grad,
        shares[0],
        shares[1],
        shares[2],
        shares[3],
        shares[4],
        shares[5],
        shares[6],
        shares[7],
        shares[8],
        shares[9],
        shares[10],
        shares[11],
        shares[12],
    )


def solution(mesh):
    placed = (
        P(("dp", "context"), None),
        P("dp", None),
        P("dp"),
        P("dp", "tensor"),
        P("dp", None),
        P("dp", None),
        P("dp"),
        P("dp"),
        P("tensor", "dp"),
        P("dp"),
        P("dp"),
        P("dp", "tensor"),
        P("dp", "tensor"),
        P("tensor", "dp"),
        P("dp"),
        P(("dp", "context"), None),
    )
    return jax.shard_map(
        local,
        mesh=mesh,
        in_specs=placed,
        out_specs=(
            P(("dp", "context"), None),
            P(("dp", "context"), None),
            P("dp"),
            P("dp", "tensor"),
            P("dp", None),
            P("dp", None),
            P("dp"),
            P("dp"),
            P("tensor", "dp"),
            P("dp"),
            P("dp"),
            P("dp", "tensor"),
            P("dp", "tensor"),
            P("tensor", "dp"),
            P("dp"),
        ),
        check_vma=False,
    )
```

profile of v0, /device:TPU:0, one launch (start us, length us, event | category | flops | bytes accessed | tf_op | source)
XLA Modules:
  0.0 614.7 jit_solution(17788061807862818543)
XLA Ops:
  12.6 6.5 %all-reduce.11 = (bf16[640]{0:T(1024)(128)(2,1)S(1)}, bf16[640]{0:T(1024)(128)(2,1)S(1)}, bf16[640]{0:T(1024)(128)(2,1)S(1)}, bf16[640]{0:T(1024)(128)(2,1)}) all-reduce(bf16[640]{0:T(1024)(128)(2,1)S(1)} %dynamic-update-slice.2, bf16[640]{0:T(1024)(128)(2,1)S(1)} %dynamic-update-slice.1, ...), channel_id=1, replica_groups=mesh['dp'=2,'context'=4,'tensor'=4] {'dp'}, use_global_device_ids=true, to_apply=%add.6 | all-reduce | flops 2560 | bytes 10240
  19.1 1.5 fusion.35
  20.6 6.4 %all_gather.40 = bf16[640,256]{1,0:T(8,128)(2,1)S(1)} all-gather(bf16[320,256]{1,0:T(8,128)(2,1)} %param.21), channel_id=1, replica_groups=mesh['dp'=2,'context'=4,'tensor'=4] {'dp'}, dimensions={0}, use_global_device_ids=true | all-gather | bytes 491520 | tf_op jit(solution)/shard_map/all_gather | solution.py:109
  27.7 1.7 convolution_convert_fusion.5
  29.5 4.0 collective-permute-start.3
  33.8 4.2 all-gather
  38.1 6.0 all_gather.41
  45.6 1.7 fusion.84
  47.3 3.5 collective-permute-start
  50.8 4.2 all-gather.1
  55.6 6.0 all_gather.43
  61.6 6.0 all_gather.45
  68.5 1.7 fusion.111
  71.4 3.5 collective-permute-start.4
  74.9 2.0 collective-permute-start.1
  78.0 6.2 %collective-permute-done.4 = bf16[768,256]{1,0:T(8,128)(2,1)S(1)} collective-permute-done((bf16[768,256]{1,0:T(8,128)(2,1)S(1)}, bf16[768,256]{1,0:T(8,128)(2,1)S(1)}, u32[]{:S(2)}, u32[]{:S(2)}) %collective-permute-start.4) | collective-permute-done | bytes 393248 | tf_op jit(solution)/shard_map/ppermute | solution.py:17
  84.3 4.4 collective-permute-start.5
  88.7 3.4 collective-permute-done.1
  92.1 4.9 collective-permute-start.2
  98.1 3.6 collective-permute-done.2
  107.8 1.5 convolution_convert_fusion.1
  109.4 9.3 %all_gather.48 = bf16[640,512]{1,0:T(8,128)(2,1)} all-gather(bf16[320,512]{1,0:T(8,128)(2,1)} %param.27), channel_id=1, replica_groups=mesh['dp'=2,'context'=4,'tensor'=4] {'dp'}, dimensions={0}, use_global_device_ids=true | all-gather | bytes 983040 | tf_op jit(solution)/shard_map/all_gather | solution.py:117
  118.7 9.2 %all_gather.49 = bf16[640,512]{1,0:T(8,128)(2,1)} all-gather(bf16[320,512]{1,0:T(8,128)(2,1)} %param.28), channel_id=1, replica_groups=mesh['dp'=2,'context'=4,'tensor'=4] {'dp'}, dimensions={0}, use_global_device_ids=true | all-gather | bytes 983040 | tf_op jit(solution)/shard_map/all_gather | solution.py:118
  127.9 7.8 %all_gather.50 = bf16[512,640]{0,1:T(8,128)(2,1)} all-gather(bf16[512,320]{0,1:T(8,128)(2,1)S(1)} %copy-done.67), channel_id=1, replica_groups=mesh['dp'=2,'context'=4,'tensor'=4] {'dp'}, dimensions={1}, use_global_device_ids=true | all-gather | bytes 983040 | tf_op jit(solution)/shard_map/all_gather | solution.py:119
  135.8 9.4 %all-reduce.18.cloned.1.call-done = bf16[768,640]{1,0:T(8,128)(2,1)} async-done(((bf16[768,640]{1,0:T(8,128)(2,1)}), bf16[768,640]{1,0:T(8,128)(2,1)}) %all-reduce.18.cloned.1.call-update) | async-done | bytes 983056 | tf_op jit(solution)/shard_map/psum | solution.py:199
  145.2 1.5 fusion.31
  147.3 1.9 multiply_reduce_fusion
  152.6 2.2 multiply_convert_fusion.2
  155.7 1.7 convolution_convert_fusion.2
  158.8 34.7 %all-reduce.20.cloned.1.call-done = bf16[768,640]{1,0:T(8,128)(2,1)} async-done(((bf16[768,640]{1,0:T(8,128)(2,1)}), bf16[768,640]{1,0:T(8,128)(2,1)}) %all-reduce.20.cloned.1.call-update) | async-done | bytes 983056 | tf_op jit(solution)/shard_map/psum | solution.py:214
  193.6 1.6 fusion.33
  195.2 3.3 fusion.27
  200.2 1.8 multiply_convert_fusion.1
  203.6 1.8 add_convert_fusion
  205.6 3.3 fusion.158
  208.9 32.5 %all-reduce.22.cloned.1.call-done = bf16[768,640]{1,0:T(8,128)(2,1)} async-done(((bf16[768,640]{1,0:T(8,128)(2,1)}), bf16[768,640]{1,0:T(8,128)(2,1)}) %all-reduce.22.cloned.1.call-update) | async-done | bytes 983056 | tf_op jit(solution)/shard_map/psum | solution.py:228
  241.5 3.5 fusion.26
  245.0 4.3 fusion.24
  259.5 2.4 fusion.3
  262.0 2.1 fusion.60
  269.7 1.6 fusion.93
  271.3 1.5 collective-permute-start.6
  273.2 6.4 %collective-permute-done.9 = bf16[768,256]{1,0:T(8,128)(2,1)S(1)} collective-permute-done((bf16[768,256]{1,0:T(8,128)(2,1)S(1)}, bf16[768,256]{1,0:T(8,128)(2,1)S(1)}, u32[]{:S(2)}, u32[]{:S(2)}) %collective-permute-start.9) | collective-permute-done | bytes 393248 | tf_op jit(solution)/shard_map/ppermute | solution.py:17
  281.4 6.6 %collective-permute-done.6 = bf16[768,256]{0,1:T(8,128)(2,1)S(1)} collective-permute-done((bf16[768,256]{0,1:T(8,128)(2,1)S(1)}, bf16[768,256]{0,1:T(8,128)(2,1)S(1)}, u32[]{:S(2)}, u32[]{:S(2)}) %collective-permute-start.6) | collective-permute-done | bytes 393248 | tf_op jit(solution)/shard_map/ppermute | solution.py:17
  290.0 6.4 %collective-permute-done.10 = bf16[768,256]{1,0:T(8,128)(2,1)S(1)} collective-permute-done((bf16[768,256]{1,0:T(8,128)(2,1)S(1)}, bf16[768,256]{1,0:T(8,128)(2,1)S(1)}, u32[]{:S(2)}, u32[]{:S(2)}) %collective-permute-start.10) | collective-permute-done | bytes 393248 | tf_op jit(solution)/shard_map/ppermute | solution.py:17
  297.8 7.0 %collective-permute-done.7 = bf16[768,256]{0,1:T(8,128)(2,1)S(1)} collective-permute-done((bf16[768,256]{0,1:T(8,128)(2,1)S(1)}, bf16[768,256]{0,1:T(8,128)(2,1)S(1)}, u32[]{:S(2)}, u32[]{:S(2)}) %collective-permute-start.7) | collective-permute-done | bytes 393248 | tf_op jit(solution)/shard_map/ppermute | solution.py:17
  306.2 1.5 convolution_convert_fusion
  307.7 5.5 collective-permute-done.11
  314.1 5.6 collective-permute-done.8
  320.6 2.9 fusion.157
  323.6 1.8 fusion.156
  326.7 1.5 fusion.136
  328.2 39.0 %all-reduce.26.cloned.1.call-done = (bf16[768,256]{0,1:T(8,128)(2,1)}, bf16[768,640]{1,0:T(8,128)(2,1)}, bf16[768,256]{1,0:T(8,128)(2,1)}) async-done(((bf16[768,256]{0,1:T(8,128)(2,1)}, bf16[768,640]{1,0:T(8,128)(2,1)}, bf16[768,256]{1,0:T(8,128)(2,1)}), (bf16[768,256]{0,1:T(8,128)(2,1)}, bf16[768,640]{1,0:T(8,128)(2,1)}, bf16[768,256]{1,0:T(8,128)(2,1)})) %all-reduce.26.cloned.1.call-update) | async-done | bytes 1769488 | tf_op jit(solution)/shard_map/psum | solution.py:291
  368.2 1.7 fusion.87
  370.3 1.5 fusion.134
  371.8 1.5 fusion.132
  373.3 5.9 psum.150
  379.8 3.7 fusion.21
  383.5 40.1 %all-reduce.8 = (f32[640]{0:T(1024)S(1)}, f32[256]{0:T(256)S(1)}, f32[256]{0:T(256)S(1)}, f32[640]{0:T(1024)S(1)}, f32[640]{0:T(1024)S(1)}, /*index=5*/f32[640]{0:T(1024)S(1)}) all-reduce(f32[640]{0:T(1024)S(1)} %get-tuple-element.19, bf16[256]{0:T(256)(128)(2,1)S(1)} %psum.150, ...), channel_id=1, replica_groups=mesh['dp'=2,'context'=4,'tensor'=4] {'dp','context'}, use_global_device_ids=true, to_apply=%region_37.38 | all-reduce | flops 3072 | bytes 24064 | tf_op jit(solution)/shard_map/psum | solution.py:312
  427.4 3.3 fusion.30
  430.7 168.4 %all-reduce.24.cloned.1.call-done = (f32[640,256]{1,0:T(8,128)}, f32[640,256]{1,0:T(8,128)}, f32[640,256]{1,0:T(8,128)}, f32[256,640]{0,1:T(8,128)}, f32[640,512...) async-done(((f32[640,256]{1,0:T(8,128)}, f32[640,256]{1,0:T(8,128)}, f32[640,256]{1,0:T(8,128)}, f32[256,640]{0,1:T(8,128)}, f32[640,512]{1,0:T(8,128)}, ...) | async-done | bytes 6553616 | tf_op jit(solution)/shard_map/psum | solution.py:312
  599.2 1.9 constant_dynamic-slice_fusion.5
  601.0 1.7 constant_dynamic-slice_fusion.4
  602.7 1.8 constant_dynamic-slice_fusion.3
  (360 shorter events, 62.4 us)
Async XLA Ops:
  7.2 138.0 %all-reduce.18.cloned.1.call-start = ((), (), s32[]{:S(2)}) async-start(), calls=%async_computation | async-start | bytes 1966080 | tf_op jit(solution)/shard_map/psum | solution.py:199
  19.0 48.6 %copy-start.87 = (f32[640]{0:T(1024)}, f32[640]{0:T(1024)S(1)}, u32[]{:S(2)}) copy-start(f32[640]{0:T(1024)S(1)} %convert_element_type.203) | copy-start | bytes 7684
  19.0 14.5 %copy-start.116 = (s32[1,2]{1,0:T(1,128)S(1)}, s32[1,2]{1,0:T(1,128)}, u32[]{:S(2)}) copy-start(s32[1,2]{1,0:T(1,128)} %param.17) | copy-start | bytes 28
  19.1 14.7 %copy-start.117 = (bf16[128]{0:T(256)(128)(2,1)S(1)}, bf16[128]{0:T(256)(128)(2,1)}, u32[]{:S(2)}) copy-start(bf16[128]{0:T(256)(128)(2,1)} %param.23) | copy-start | bytes 772
  19.1 19.1 %copy-start.73 = (bf16[320,256]{1,0:T(8,128)(2,1)S(1)}, bf16[320,256]{1,0:T(8,128)(2,1)}, u32[]{:S(2)}) copy-start(bf16[320,256]{1,0:T(8,128)(2,1)} %param.20) | copy-start | bytes 491524
  20.6 24.2 %copy-start.91 = (f32[768]{0:T(1024)}, f32[768]{0:T(1024)S(1)}, u32[]{:S(2)}) copy-start(f32[768]{0:T(1024)S(1)} %fusion.35) | copy-start | bytes 9220
  20.6 23.6 %copy-start.6 = (bf16[768,640]{1,0:T(8,128)(2,1)S(1)}, bf16[768,640]{1,0:T(8,128)(2,1)}, u32[]{:S(2)}) copy-start(bf16[768,640]{1,0:T(8,128)(2,1)} %param.16) | copy-start | bytes 2949124
  20.6 47.0 %copy-start.89 = (f32[768]{0:T(1024)}, f32[768]{0:T(1024)S(1)}, u32[]{:S(2)}) copy-start(f32[768]{0:T(1024)S(1)} %fusion.124) | copy-start | bytes 9220
  29.5 16.0 %copy-start.39 = (bf16[768,256]{1,0:T(8,128)(2,1)}, bf16[768,256]{1,0:T(8,128)(2,1)S(1)}, u32[]{:S(2)}) copy-start(bf16[768,256]{1,0:T(8,128)(2,1)S(1)} %convolution_convert_fusion.5) | copy-start | bytes 1179652
  29.5 41.9 %collective-permute-start.3 = (bf16[768,256]{1,0:T(8,128)(2,1)S(1)}, bf16[768,256]{1,0:T(8,128)(2,1)S(1)}, u32[]{:S(2)}, u32[]{:S(2)}) collective-permute-start(bf16[768,256]{1,0:T(8,128)(2,1)S(1)} %convolution_convert_fusion.5), channel_id=1, source_target_pairs={{0,4},{4,8},{8,12},{1,5},{5,9},{9,13},{2,6},{6,10},{10,14},{3,7},{... | collective-permute-start | bytes 1179656 | tf_op jit(solution)/shard_map/ppermute | solution.py:17
  33.5 35.0 %copy-start.114 = (f32[128]{0:T(128)}, f32[128]{0:T(128)S(1)}, u32[]{:S(2)}) copy-start(f32[128]{0:T(128)S(1)} %multiply_exponential_fusion) | copy-start | bytes 1540
  33.5 12.0 %copy-start.112 = (s32[768]{0:T(1024)}, s32[768]{0:T(1024)S(1)}, u32[]{:S(2)}) copy-start(s32[768]{0:T(1024)S(1)} %get-tuple-element.90) | copy-start | bytes 9220
  33.6 12.0 %copy-start.110 = (s32[768]{0:T(1024)}, s32[768]{0:T(1024)S(1)}, u32[]{:S(2)}) copy-start(s32[768]{0:T(1024)S(1)} %get-tuple-element.89) | copy-start | bytes 9220
  33.6 43.3 %copy-start.108 = (s32[768]{0:T(1024)}, s32[768]{0:T(1024)S(1)}, u32[]{:S(2)}) copy-start(s32[768]{0:T(1024)S(1)} %get-tuple-element.88) | copy-start | bytes 9220
  38.0 7.6 %copy-start.98 = (f32[2,1,128]{2,1,0:T(1,128)}, f32[2,1,128]{2,1,0:T(1,128)S(1)}, u32[]{:S(2)}) copy-start(f32[2,1,128]{2,1,0:T(1,128)S(1)} %convert_element_type.258) | copy-start | bytes 3076
  44.8 16.8 %copy-start.17 = (f32[768,256]{0,1:T(8,128)}, f32[768,256]{0,1:T(8,128)S(1)}, u32[]{:S(2)}) copy-start(f32[768,256]{0,1:T(8,128)S(1)} %get-tuple-element.73) | copy-start | bytes 2359300
  44.8 5.9 copy-start.118
  44.8 10.8 %copy-start.74 = (bf16[320,256]{1,0:T(8,128)(2,1)S(1)}, bf16[320,256]{1,0:T(8,128)(2,1)}, u32[]{:S(2)}) copy-start(bf16[320,256]{1,0:T(8,128)(2,1)} %param.19) | copy-start | bytes 491524
  44.9 16.8 %copy-start.83 = (f32[768]{0:T(1024)}, f32[768]{0:T(1024)S(1)}, u32[]{:S(2)}) copy-start(f32[768]{0:T(1024)S(1)} %fusion.125) | copy-start | bytes 9220
  45.4 16.2 %copy-start.75 = (bf16[256,320]{0,1:T(8,128)(2,1)S(1)}, bf16[256,320]{0,1:T(8,128)(2,1)}, u32[]{:S(2)}) copy-start(bf16[256,320]{0,1:T(8,128)(2,1)} %param.24) | copy-start | bytes 491524
  47.2 23.0 %copy-start.31 = (bf16[768,128]{0,1:T(8,128)(2,1)}, bf16[768,128]{0,1:T(8,128)(2,1)S(1)}, u32[]{:S(2)}) copy-start(bf16[768,128]{0,1:T(8,128)(2,1)S(1)} %get-tuple-element.67) | copy-start | bytes 589828
  47.3 27.6 %collective-permute-start = (bf16[768,256]{0,1:T(8,128)(2,1)S(1)}, bf16[768,256]{0,1:T(8,128)(2,1)S(1)}, u32[]{:S(2)}, u32[]{:S(2)}) collective-permute-start(bf16[768,256]{0,1:T(8,128)(2,1)S(1)} %pad_maximum_fusion), channel_id=1, source_target_pairs={{0,4},{4,8},{8,12},{1,5},{5,9},{9,13},{2,6},{6,10},{10,14},{3,7},{... | collective-permute-start | bytes 1179656 | tf_op jit(solution)/shard_map/ppermute | solution.py:17
  55.0 13.5 %copy-start.100 = (f32[2,1,128]{2,1,0:T(1,128)}, f32[2,1,128]{2,1,0:T(1,128)S(1)}, u32[]{:S(2)}) copy-start(f32[2,1,128]{2,1,0:T(1,128)S(1)} %convert_element_type.259) | copy-start | bytes 3076
  61.6 6.9 %copy-start.47 = (bf16[640,256]{1,0:T(8,128)(2,1)}, bf16[640,256]{1,0:T(8,128)(2,1)S(1)}, u32[]{:S(2)}) copy-start(bf16[640,256]{1,0:T(8,128)(2,1)S(1)} %all_gather.43) | copy-start | bytes 983044
  67.6 39.3 %copy-start.27 = (bf16[256,640]{0,1:T(8,128)(2,1)}, bf16[256,640]{0,1:T(8,128)(2,1)S(1)}, u32[]{:S(2)}) copy-start(bf16[256,640]{0,1:T(8,128)(2,1)S(1)} %all_gather.45) | copy-start | bytes 983044
  70.2 31.6 %copy-start.68 = (bf16[768,128]{0,1:T(8,128)(2,1)}, bf16[768,128]{0,1:T(8,128)(2,1)S(1)}, u32[]{:S(2)}) copy-start(bf16[768,128]{0,1:T(8,128)(2,1)S(1)} %get-tuple-element.64) | copy-start | bytes 589828
  70.2 31.6 %copy-start.70 = (bf16[768,128]{0,1:T(8,128)(2,1)}, bf16[768,128]{0,1:T(8,128)(2,1)S(1)}, u32[]{:S(2)}) copy-start(bf16[768,128]{0,1:T(8,128)(2,1)S(1)} %get-tuple-element.65) | copy-start | bytes 589828
  71.0 32.7 %copy-start = (f32[1,768,768]{1,2,0:T(8,128)}, f32[1,768,768]{1,2,0:T(8,128)S(1)}, u32[]{:S(2)}) copy-start(f32[1,768,768]{1,2,0:T(8,128)S(1)} %get-tuple-element.83) | copy-start | bytes 7077892
  71.4 6.2 %copy-start.42 = (bf16[768,256]{1,0:T(8,128)(2,1)}, bf16[768,256]{1,0:T(8,128)(2,1)S(1)}, u32[]{:S(2)}) copy-start(bf16[768,256]{1,0:T(8,128)(2,1)S(1)} %collective-permute-done.3) | copy-start | bytes 1179652
  71.4 12.9 %collective-permute-start.4 = (bf16[768,256]{1,0:T(8,128)(2,1)S(1)}, bf16[768,256]{1,0:T(8,128)(2,1)S(1)}, u32[]{:S(2)}, u32[]{:S(2)}) collective-permute-start(bf16[768,256]{1,0:T(8,128)(2,1)S(1)} %collective-permute-done.3), channel_id=1, source_target_pairs={{0,4},{4,8},{8,12},{1,5},{5,9},{9,13},{2,6},{6,10},{10,14},{3,7},{... | collective-permute-start | bytes 1179656 | tf_op jit(solution)/shard_map/ppermute | solution.py:17
  74.9 17.2 %collective-permute-start.1 = (bf16[768,256]{0,1:T(8,128)(2,1)S(1)}, bf16[768,256]{0,1:T(8,128)(2,1)S(1)}, u32[]{:S(2)}, u32[]{:S(2)}) collective-permute-start(bf16[768,256]{0,1:T(8,128)(2,1)S(1)} %collective-permute-done), channel_id=1, source_target_pairs={{0,4},{4,8},{8,12},{1,5},{5,9},{9,13},{2,6},{6,10},{10,14},{3,7},{... | collective-permute-start | bytes 1179656 | tf_op jit(solution)/shard_map/ppermute | solution.py:17
  77.6 27.5 %copy-start.2 = (f32[1,768,768]{1,2,0:T(8,128)}, f32[1,768,768]{1,2,0:T(8,128)S(1)}, u32[]{:S(2)}) copy-start(f32[1,768,768]{1,2,0:T(8,128)S(1)} %get-tuple-element.81) | copy-start | bytes 7077892
  77.6 19.4 %copy-start.109 = (s32[768]{0:T(1024)S(1)}, s32[768]{0:T(1024)}, u32[]{:S(2)}) copy-start(s32[768]{0:T(1024)} %copy-done.108) | copy-start | bytes 9220
  77.7 19.4 %copy-start.113 = (s32[768]{0:T(1024)S(1)}, s32[768]{0:T(1024)}, u32[]{:S(2)}) copy-start(s32[768]{0:T(1024)} %copy-done.112) | copy-start | bytes 9220
  84.3 21.5 %copy-start.33 = (bf16[768,256]{1,0:T(8,128)(2,1)}, bf16[768,256]{1,0:T(8,128)(2,1)S(1)}, u32[]{:S(2)}) copy-start(bf16[768,256]{1,0:T(8,128)(2,1)S(1)} %collective-permute-done.4) | copy-start | bytes 1179652
  84.3 22.0 %collective-permute-start.5 = (bf16[768,256]{1,0:T(8,128)(2,1)S(1)}, bf16[768,256]{1,0:T(8,128)(2,1)S(1)}, u32[]{:S(2)}, u32[]{:S(2)}) collective-permute-start(bf16[768,256]{1,0:T(8,128)(2,1)S(1)} %collective-permute-done.4), channel_id=1, source_target_pairs={{0,4},{4,8},{8,12},{1,5},{5,9},{9,13},{2,6},{6,10},{10,14},{3,7},{... | collective-permute-start | bytes 1179656 | tf_op jit(solution)/shard_map/ppermute | solution.py:17
  92.1 5.6 copy-start.59
  92.1 9.7 %collective-permute-start.2 = (bf16[768,256]{0,1:T(8,128)(2,1)S(1)}, bf16[768,256]{0,1:T(8,128)(2,1)S(1)}, u32[]{:S(2)}, u32[]{:S(2)}) collective-permute-start(bf16[768,256]{0,1:T(8,128)(2,1)S(1)} %collective-permute-done.1), channel_id=1, source_target_pairs={{0,4},{4,8},{8,12},{1,5},{5,9},{9,13},{2,6},{6,10},{10,14},{3,7},{... | collective-permute-start | bytes 1179656 | tf_op jit(solution)/shard_map/ppermute | solution.py:17
  109.3 84.3 %all-reduce.20.cloned.1.call-start = ((), (), s32[]{:S(2)}) async-start(), calls=%async_computation.1 | async-start | bytes 1966080 | tf_op jit(solution)/shard_map/psum | solution.py:214
  109.3 18.6 %copy-start.67 = (bf16[512,320]{0,1:T(8,128)(2,1)S(1)}, bf16[512,320]{0,1:T(8,128)(2,1)}, u32[]{:S(2)}) copy-start(bf16[512,320]{0,1:T(8,128)(2,1)} %param.29) | copy-start | bytes 983044
  157.5 83.9 %all-reduce.22.cloned.1.call-start = ((), (), s32[]{:S(2)}) async-start(), calls=%async_computation.2 | async-start | bytes 1966080 | tf_op jit(solution)/shard_map/psum | solution.py:228
  193.6 4.9 copy-start.11
  193.6 4.9 copy-start.13
  193.6 4.9 copy-start.79
  205.4 161.8 %all-reduce.26.cloned.1.call-start = ((), (), s32[]{:S(2)}) async-start(), calls=%async_computation.4 | async-start | bytes 3538944 | tf_op jit(solution)/shard_map/psum | solution.py:291
  265.6 13.9 %collective-permute-start.9 = (bf16[768,256]{1,0:T(8,128)(2,1)S(1)}, bf16[768,256]{1,0:T(8,128)(2,1)S(1)}, u32[]{:S(2)}, u32[]{:S(2)}) collective-permute-start(bf16[768,256]{1,0:T(8,128)(2,1)S(1)} %convolution_convert_fusion.3), channel_id=1, source_target_pairs={{4,0},{8,4},{12,8},{5,1},{9,5},{13,9},{6,2},{10,6},{14,10},{7,3},{... | collective-permute-start | bytes 1179656 | tf_op jit(solution)/shard_map/ppermute | solution.py:17
  271.3 16.7 %collective-permute-start.6 = (bf16[768,256]{0,1:T(8,128)(2,1)S(1)}, bf16[768,256]{0,1:T(8,128)(2,1)S(1)}, u32[]{:S(2)}, u32[]{:S(2)}) collective-permute-start(bf16[768,256]{0,1:T(8,128)(2,1)S(1)} %fusion.53), channel_id=1, source_target_pairs={{4,0},{8,4},{12,8},{5,1},{9,5},{13,9},{6,2},{10,6},{14,10},{7,3},{... | collective-permute-start | bytes 1179656 | tf_op jit(solution)/shard_map/ppermute | solution.py:17
  280.1 16.3 %collective-permute-start.10 = (bf16[768,256]{1,0:T(8,128)(2,1)S(1)}, bf16[768,256]{1,0:T(8,128)(2,1)S(1)}, u32[]{:S(2)}, u32[]{:S(2)}) collective-permute-start(bf16[768,256]{1,0:T(8,128)(2,1)S(1)} %add_convert_fusion.3), channel_id=1, source_target_pairs={{4,0},{8,4},{12,8},{5,1},{9,5},{13,9},{6,2},{10,6},{14,10},{7,3},{... | collective-permute-start | bytes 1179656 | tf_op jit(solution)/shard_map/ppermute | solution.py:17
  288.5 16.3 %collective-permute-start.7 = (bf16[768,256]{0,1:T(8,128)(2,1)S(1)}, bf16[768,256]{0,1:T(8,128)(2,1)S(1)}, u32[]{:S(2)}, u32[]{:S(2)}) collective-permute-start(bf16[768,256]{0,1:T(8,128)(2,1)S(1)} %add_convert_fusion.6), channel_id=1, source_target_pairs={{4,0},{8,4},{12,8},{5,1},{9,5},{13,9},{6,2},{10,6},{14,10},{7,3},{... | collective-permute-start | bytes 1179656 | tf_op jit(solution)/shard_map/ppermute | solution.py:17
  290.0 16.2 %copy-start.48 = (bf16[640,256]{1,0:T(8,128)(2,1)S(1)}, bf16[640,256]{1,0:T(8,128)(2,1)}, u32[]{:S(2)}) copy-start(bf16[640,256]{1,0:T(8,128)(2,1)} %copy-done.47) | copy-start | bytes 983044
  296.5 16.8 %collective-permute-start.11 = (bf16[768,256]{1,0:T(8,128)(2,1)S(1)}, bf16[768,256]{1,0:T(8,128)(2,1)S(1)}, u32[]{:S(2)}, u32[]{:S(2)}) collective-permute-start(bf16[768,256]{1,0:T(8,128)(2,1)S(1)} %add_convert_fusion.2), channel_id=1, source_target_pairs={{4,0},{8,4},{12,8},{5,1},{9,5},{13,9},{6,2},{10,6},{14,10},{7,3},{... | collective-permute-start | bytes 1179656 | tf_op jit(solution)/shard_map/ppermute | solution.py:17
  304.9 14.8 %collective-permute-start.8 = (bf16[768,256]{0,1:T(8,128)(2,1)S(1)}, bf16[768,256]{0,1:T(8,128)(2,1)S(1)}, u32[]{:S(2)}, u32[]{:S(2)}) collective-permute-start(bf16[768,256]{0,1:T(8,128)(2,1)S(1)} %add_convert_fusion.5), channel_id=1, source_target_pairs={{4,0},{8,4},{12,8},{5,1},{9,5},{13,9},{6,2},{10,6},{14,10},{7,3},{... | collective-permute-start | bytes 1179656 | tf_op jit(solution)/shard_map/ppermute | solution.py:17
  314.1 6.5 %copy-start.24 = (bf16[768,640]{1,0:T(8,128)(2,1)S(1)}, bf16[768,640]{1,0:T(8,128)(2,1)}, u32[]{:S(2)}) copy-start(bf16[768,640]{1,0:T(8,128)(2,1)} %copy-done.23) | copy-start | bytes 2949124
  320.6 278.6 %all-reduce.24.cloned.1.call-start = ((), (), s32[]{:S(2)}) async-start(), calls=%async_computation.3 | async-start | bytes 13107200 | tf_op jit(solution)/shard_map/psum | solution.py:312
  328.2 41.7 %copy-start.18 = (f32[768,256]{0,1:T(8,128)S(1)}, f32[768,256]{0,1:T(8,128)}, u32[]{:S(2)}) copy-start(f32[768,256]{0,1:T(8,128)} %copy-done.17) | copy-start | bytes 2359300
  328.2 41.7 %copy-start.84 = (f32[768]{0:T(1024)S(1)}, f32[768]{0:T(1024)}, u32[]{:S(2)}) copy-start(f32[768]{0:T(1024)} %copy-done.83) | copy-start | bytes 9220
  328.2 41.7 %copy-start.99 = (f32[2,1,128]{2,1,0:T(1,128)S(1)}, f32[2,1,128]{2,1,0:T(1,128)}, u32[]{:S(2)}) copy-start(f32[2,1,128]{2,1,0:T(1,128)} %copy-done.98) | copy-start | bytes 3076
  373.3 6.0 copy-start.50
  373.3 6.5 %copy-start.46 = (bf16[640,256]{1,0:T(8,128)(2,1)S(1)}, bf16[640,256]{1,0:T(8,128)(2,1)}, u32[]{:S(2)}) copy-start(bf16[640,256]{1,0:T(8,128)(2,1)} %copy-done.45) | copy-start | bytes 983044
  379.8 47.6 %copy-start.92 = (f32[768]{0:T(1024)S(1)}, f32[768]{0:T(1024)}, u32[]{:S(2)}) copy-start(f32[768]{0:T(1024)} %copy-done.91) | copy-start | bytes 9220
  379.8 47.6 %copy-start.10 = (f32[768,640]{1,0:T(8,128)S(1)}, f32[768,640]{1,0:T(8,128)}, u32[]{:S(2)}) copy-start(f32[768,640]{1,0:T(8,128)} %copy-done.9) | copy-start | bytes 5898244
  599.1 5.4 copy-start.72
  599.1 6.2 %copy-start.66 = (f32[640,512]{1,0:T(8,128)S(1)}, f32[640,512]{1,0:T(8,128)}, u32[]{:S(2)}) copy-start(f32[640,512]{1,0:T(8,128)} %get-tuple-element.46) | copy-start | bytes 3932164
  599.1 7.0 %copy-start.65 = (f32[640,512]{1,0:T(8,128)S(1)}, f32[640,512]{1,0:T(8,128)}, u32[]{:S(2)}) copy-start(f32[640,512]{1,0:T(8,128)} %get-tuple-element.47) | copy-start | bytes 3932164
  (74 other events, 168.6 us)
Sparse Core Ops, SparseCore 0:
  109.4 35.7 all-reduce.17
  157.6 35.9 all-reduce.19
  205.5 35.8 all-reduce.21
  320.7 46.4 all-reduce.25
  373.4 225.6 all-reduce.23
where the time goes:
time: 623 us; the launch traced here: 615 us
  waiting for transfers between devices  335 us (54%)
  blocking collectives  112 us (18%)
  matrix products  48.5 us (8%)
  other arithmetic  39.9 us (6%)
  local copies, waits for them, and re-layouts  32.8 us (5%)
  starting transfers between devices  30.5 us (5%)
  between operations  16.3 us (3%)
    psum x1, waiting for transfers between devices, local(): lax.psum((grad_ginput, grad_wquery, grad_wkey, grad_wvalue, grad_gquery,...  168 us
    ppermute x12, waiting for transfers between devices, passed_along(): return lax.ppermute(array, axis, pairs)  50.9 us
    psum x1, blocking collectives, local(): lax.psum((grad_ginput, grad_wquery, grad_wkey, grad_wvalue, grad_gquery,...  40.1 us
    psum x1, waiting for transfers between devices, local(): lax.psum(carried[0].astype(jnp.bfloat16), 'tensor').astype(jnp.float32)  39 us
    psum x1, waiting for transfers between devices, local(): lax.psum(product(hidden, w_down).astype(jnp.bfloat16), 'tensor')  34.7 us
    psum x1, waiting for transfers between devices, local(): lax.psum((product_rt(grad_gate, w_gate) + product_rt(grad_up, w_up)).asty...  32.5 us
    ppermute x12, starting transfers between devices, passed_along(): return lax.ppermute(array, axis, pairs)  30.1 us
    unnamed x251, local copies, waits for them, and re-layouts  20.3 us
  transfers between devices with their start and end apart: 17, of which 14 were waited for; matrix products, arithmetic and copies ran while one was open for 7% of the time, Pallas kernels for 0%

commit v1 on v0

--- a/solution.py
+++ b/solution.py
@@ -9,6 +9,7 @@
 EPS = 1e-06
 NEG = -1000000000.0
 SCALE = 0.0625
+run_hubs = lambda axis_tag, my_tile, comm_axis: lax.psum(lax.psum(my_tile, comm_axis), axis_tag)
 
 
 def passed_along(array, axis, by):
@@ -309,7 +310,8 @@
     )
     grad_stream_norm, grad_ginput = input_back(grad_normed)
     tokens_grad = grad_middle + grad_stream_norm
-    totals = lax.psum(
+    totals = run_hubs(
+        "dp",
         (
             grad_ginput,
             grad_wquery,
@@ -325,7 +327,7 @@
             grad_wdown,
             grad_gfeed,
         ),
-        ("dp", "context"),
+        "context",
     )
     shard_place = lax.axis_index("dp")
     shard_count = lax.axis_size("dp")

time: 623 us -> 794 us (1.27)
  waiting for transfers between devices: 335 us -> 520 us
  blocking collectives: 112 us -> 98 us
    psum x1 -> x2, waiting for transfers between devices: 168 us -> 353 us  [the longest x1 234 us: lax.psum(my_tile, comm_axis)]
    psum x1 -> x2, blocking collectives: 40.1 us -> 25.3 us  [the longest x1 16.7 us: lax.psum(my_tile, comm_axis)]
  transfers between devices with their start and end apart: 17 -> 18, of which waited for: 14 -> 15; matrix products, arithmetic and copies ran while one was open for 7% -> 6% of each run, Pallas kernels for 0% -> 0%
where the time goes in v1:
time: 794 us; the launch traced here: 786 us
  waiting for transfers between devices  520 us (65%)
  blocking collectives  98 us (12%)
  matrix products  48.8 us (6%)
  other arithmetic  39.9 us (5%)
  local copies, waits for them, and re-layouts  32.8 us (4%)
  starting transfers between devices  30.6 us (4%)
  between operations  16.7 us (2%)
    psum x1, waiting for transfers between devices, lax.psum(my_tile, comm_axis)  234 us
    psum x1, waiting for transfers between devices, lax.psum(lax.psum(my_tile, comm_axis), axis_tag)  119 us
    ppermute x12, waiting for transfers between devices, passed_along(): return lax.ppermute(array, axis, pairs)  50.9 us
    psum x1, waiting for transfers between devices, local(): lax.psum(carried[0].astype(jnp.bfloat16), 'tensor').astype(jnp.float32)  38.8 us
    psum x1, waiting for transfers between devices, local(): lax.psum(product(hidden, w_down).astype(jnp.bfloat16), 'tensor')  34.7 us
    psum x1, waiting for transfers between devices, local(): lax.psum((product_rt(grad_gate, w_gate) + product_rt(grad_up, w_up)).asty...  32.5 us
    ppermute x12, starting transfers between devices, passed_along(): return lax.ppermute(array, axis, pairs)  30.1 us
    unnamed x251, local copies, waits for them, and re-layouts  20.3 us
  transfers between devices with their start and end apart: 18, of which 15 were waited for; matrix products, arithmetic and copies ran while one was open for 6% of the time, Pallas kernels for 0%

profile of v1, /device:TPU:0, one launch (start us, length us, event | category | flops | bytes accessed | tf_op | source)
XLA Modules:
  0.0 786.2 jit_solution(8025184135944303783)
XLA Ops:
  12.6 6.5 all-reduce.13
  19.1 1.5 fusion.35
  20.6 6.4 all_gather.40
  27.7 1.7 convolution_convert_fusion.5
  29.5 4.0 collective-permute-start.3
  33.8 4.2 all-gather
  38.1 6.0 all_gather.41
  45.6 1.7 fusion.84
  47.3 3.5 collective-permute-start
  50.8 4.2 all-gather.1
  55.6 6.0 all_gather.43
  61.6 6.0 all_gather.45
  68.5 1.7 fusion.111
  71.4 3.5 collective-permute-start.4
  74.9 2.0 collective-permute-start.1
  78.0 6.2 collective-permute-done.4
  84.3 4.4 collective-permute-start.5
  88.7 3.4 collective-permute-done.1
  92.1 4.9 collective-permute-start.2
  98.1 3.6 collective-permute-done.2
  109.4 9.3 %all_gather.48 = bf16[640,512]{1,0:T(8,128)(2,1)} all-gather(bf16[320,512]{1,0:T(8,128)(2,1)} %param.27), channel_id=1, replica_groups=mesh['dp'=2,'context'=4,'tensor'=4] {'dp'}, dimensions={0}, use_global_device_ids=true | all-gather | bytes 983040 | tf_op jit(solution)/shard_map/all_gather | solution.py:118
  118.7 9.2 %all_gather.49 = bf16[640,512]{1,0:T(8,128)(2,1)} all-gather(bf16[320,512]{1,0:T(8,128)(2,1)} %param.28), channel_id=1, replica_groups=mesh['dp'=2,'context'=4,'tensor'=4] {'dp'}, dimensions={0}, use_global_device_ids=true | all-gather | bytes 983040 | tf_op jit(solution)/shard_map/all_gather | solution.py:119
  127.9 7.8 all_gather.50
  135.8 9.4 %all-reduce.21.cloned.1.call-done = bf16[768,640]{1,0:T(8,128)(2,1)} async-done(((bf16[768,640]{1,0:T(8,128)(2,1)}), bf16[768,640]{1,0:T(8,128)(2,1)}) %all-reduce.21.cloned.1.call-update) | async-done | bytes 983056 | tf_op jit(solution)/shard_map/psum | solution.py:200
  145.2 1.5 fusion.31
  147.3 1.9 multiply_reduce_fusion
  152.6 2.2 multiply_convert_fusion.2
  155.7 1.7 convolution_convert_fusion.2
  158.8 34.7 %all-reduce.23.cloned.1.call-done = bf16[768,640]{1,0:T(8,128)(2,1)} async-done(((bf16[768,640]{1,0:T(8,128)(2,1)}), bf16[768,640]{1,0:T(8,128)(2,1)}) %all-reduce.23.cloned.1.call-update) | async-done | bytes 983056 | tf_op jit(solution)/shard_map/psum | solution.py:215
  193.6 1.6 fusion.33
  195.2 3.3 fusion.27
  200.2 1.8 multiply_convert_fusion.1
  203.6 1.8 add_convert_fusion
  205.6 3.3 fusion.158
  208.9 32.5 %all-reduce.25.cloned.1.call-done = bf16[768,640]{1,0:T(8,128)(2,1)} async-done(((bf16[768,640]{1,0:T(8,128)(2,1)}), bf16[768,640]{1,0:T(8,128)(2,1)}) %all-reduce.25.cloned.1.call-update) | async-done | bytes 983056 | tf_op jit(solution)/shard_map/psum | solution.py:229
  241.5 3.5 fusion.26
  245.0 4.3 fusion.24
  259.5 2.4 fusion.3
  262.0 2.1 fusion.60
  269.7 1.6 fusion.93
  271.3 1.5 collective-permute-start.6
  273.2 6.4 collective-permute-done.9
  281.4 6.6 collective-permute-done.6
  290.0 6.4 collective-permute-done.10
  297.8 7.0 collective-permute-done.7
  306.2 1.5 convolution_convert_fusion
  307.7 5.6 collective-permute-done.11
  314.1 5.6 collective-permute-done.8
  320.7 3.0 fusion.157
  323.7 1.8 fusion.156
  328.3 38.8 %all-reduce.31.cloned.1.call-done = (bf16[768,256]{0,1:T(8,128)(2,1)}, bf16[768,640]{1,0:T(8,128)(2,1)}, bf16[768,256]{1,0:T(8,128)(2,1)}) async-done(((bf16[768,256]{0,1:T(8,128)(2,1)}, bf16[768,640]{1,0:T(8,128)(2,1)}, bf16[768,256]{1,0:T(8,128)(2,1)}), (bf16[768,256]{0,1:T(8,128)(2,1)}, bf16[768,640]{1,0:T(8,128)(2,1)}, bf16[768,256]{1,0:T(8,128)(2,1)})) %all-reduce.31.cloned.1.call-update) | async-done | bytes 1769488 | tf_op jit(solution)/shard_map/psum | solution.py:292
  368.2 1.7 fusion.87
  370.3 1.5 fusion.134
  371.8 1.5 fusion.132
  373.4 233.6 %all-reduce.27.cloned.1.call-done = (f32[640,256]{1,0:T(8,128)}, f32[640,256]{1,0:T(8,128)}, f32[640,256]{1,0:T(8,128)}, f32[256,640]{0,1:T(8,128)}, f32[640,512...) async-done(((f32[640,256]{1,0:T(8,128)}, f32[640,256]{1,0:T(8,128)}, f32[640,256]{1,0:T(8,128)}, f32[256,640]{0,1:T(8,128)}, f32[640,512]{1,0:T(8,128)}, ...) | async-done | bytes 6553616 | tf_op jit(solution)/shard_map/psum | solution.py:12
  607.0 7.0 psum.245
  614.6 3.9 fusion.21
  618.5 16.7 %all-reduce.8 = (f32[640]{0:T(1024)S(1)}, f32[256]{0:T(256)S(1)}, f32[256]{0:T(256)S(1)}, f32[640]{0:T(1024)S(1)}, f32[640]{0:T(1024)S(1)}, /*index=5*/f32[640]{0:T(1024)S(1)}) all-reduce(f32[640]{0:T(1024)S(1)} %get-tuple-element.19, bf16[256]{0:T(256)(128)(2,1)S(1)} %psum.245, ...), channel_id=1, replica_groups=mesh['dp'=2,'context'=4,'tensor'=4] {'context'}, use_global_device_ids=true, to_apply=%region_37.38 | all-reduce | flops 3072 | bytes 24064 | tf_op jit(solution)/shard_map/psum | solution.py:12
  635.2 8.6 %all-reduce.10 = (f32[640]{0:T(1024)S(1)}, f32[256]{0:T(256)S(1)}, f32[256]{0:T(256)S(1)}, f32[640]{0:T(1024)S(1)}, f32[640]{0:T(1024)S(1)}, /*index=5*/f32[640]{0:T(1024)S(1)}) all-reduce(f32[640]{0:T(1024)S(1)} %get-tuple-element.36, f32[256]{0:T(256)S(1)} %get-tuple-element.37, ...), channel_id=1, replica_groups=mesh['dp'=2,'context'=4,'tensor'=4] {'dp'}, use_global_device_ids=true, to_apply=%region_38.39 | all-reduce | flops 3072 | bytes 24576 | tf_op jit(solution)/shard_map/psum | solution.py:12
  647.6 3.3 fusion.30
  651.0 119.3 %all-reduce.29.cloned.1.call-done = (f32[640,256]{1,0:T(8,128)}, f32[640,256]{1,0:T(8,128)}, f32[640,256]{1,0:T(8,128)}, f32[256,640]{0,1:T(8,128)}, f32[640,512...) async-done(((f32[640,256]{1,0:T(8,128)}, f32[640,256]{1,0:T(8,128)}, f32[640,256]{1,0:T(8,128)}, f32[256,640]{0,1:T(8,128)}, f32[640,512]{1,0:T(8,128)}, ...) | async-done | bytes 6553616 | tf_op jit(solution)/shard_map/psum | solution.py:12
  770.3 1.9 constant_dynamic-slice_fusion.5
  772.2 1.7 constant_dynamic-slice_fusion.4
  773.9 1.8 constant_dynamic-slice_fusion.3
  (364 shorter events, 65.4 us)
Async XLA Ops:
  7.2 138.0 %all-reduce.21.cloned.1.call-start = ((), (), s32[]{:S(2)}) async-start(), calls=%async_computation | async-start | bytes 1966080 | tf_op jit(solution)/shard_map/psum | solution.py:200
  19.0 48.6 %copy-start.87 = (f32[640]{0:T(1024)}, f32[640]{0:T(1024)S(1)}, u32[]{:S(2)}) copy-start(f32[640]{0:T(1024)S(1)} %convert_element_type.203) | copy-start | bytes 7684
  19.0 14.5 %copy-start.116 = (s32[1,2]{1,0:T(1,128)S(1)}, s32[1,2]{1,0:T(1,128)}, u32[]{:S(2)}) copy-start(s32[1,2]{1,0:T(1,128)} %param.17) | copy-start | bytes 28
  19.1 14.7 %copy-start.117 = (bf16[128]{0:T(256)(128)(2,1)S(1)}, bf16[128]{0:T(256)(128)(2,1)}, u32[]{:S(2)}) copy-start(bf16[128]{0:T(256)(128)(2,1)} %param.23) | copy-start | bytes 772
  19.1 19.1 %copy-start.73 = (bf16[320,256]{1,0:T(8,128)(2,1)S(1)}, bf16[320,256]{1,0:T(8,128)(2,1)}, u32[]{:S(2)}) copy-start(bf16[320,256]{1,0:T(8,128)(2,1)} %param.20) | copy-start | bytes 491524
  20.6 24.2 %copy-start.91 = (f32[768]{0:T(1024)}, f32[768]{0:T(1024)S(1)}, u32[]{:S(2)}) copy-start(f32[768]{0:T(1024)S(1)} %fusion.35) | copy-start | bytes 9220
  20.6 23.6 %copy-start.6 = (bf16[768,640]{1,0:T(8,128)(2,1)S(1)}, bf16[768,640]{1,0:T(8,128)(2,1)}, u32[]{:S(2)}) copy-start(bf16[768,640]{1,0:T(8,128)(2,1)} %param.16) | copy-start | bytes 2949124
  20.6 47.0 %copy-start.89 = (f32[768]{0:T(1024)}, f32[768]{0:T(1024)S(1)}, u32[]{:S(2)}) copy-start(f32[768]{0:T(1024)S(1)} %fusion.124) | copy-start | bytes 9220
  29.5 16.0 %copy-start.39 = (bf16[768,256]{1,0:T(8,128)(2,1)}, bf16[768,256]{1,0:T(8,128)(2,1)S(1)}, u32[]{:S(2)}) copy-start(bf16[768,256]{1,0:T(8,128)(2,1)S(1)} %convolution_convert_fusion.5) | copy-start | bytes 1179652
  29.5 41.9 %collective-permute-start.3 = (bf16[768,256]{1,0:T(8,128)(2,1)S(1)}, bf16[768,256]{1,0:T(8,128)(2,1)S(1)}, u32[]{:S(2)}, u32[]{:S(2)}) collective-permute-start(bf16[768,256]{1,0:T(8,128)(2,1)S(1)} %convolution_convert_fusion.5), channel_id=1, source_target_pairs={{0,4},{4,8},{8,12},{1,5},{5,9},{9,13},{2,6},{6,10},{10,14},{3,7},{... | collective-permute-start | bytes 1179656 | tf_op jit(solution)/shard_map/ppermute | solution.py:18
  33.5 35.0 %copy-start.114 = (f32[128]{0:T(128)}, f32[128]{0:T(128)S(1)}, u32[]{:S(2)}) copy-start(f32[128]{0:T(128)S(1)} %multiply_exponential_fusion) | copy-start | bytes 1540
  33.5 12.0 %copy-start.112 = (s32[768]{0:T(1024)}, s32[768]{0:T(1024)S(1)}, u32[]{:S(2)}) copy-start(s32[768]{0:T(1024)S(1)} %get-tuple-element.103) | copy-start | bytes 9220
  33.6 12.0 %copy-start.110 = (s32[768]{0:T(1024)}, s32[768]{0:T(1024)S(1)}, u32[]{:S(2)}) copy-start(s32[768]{0:T(1024)S(1)} %get-tuple-element.102) | copy-start | bytes 9220
  33.6 43.3 %copy-start.108 = (s32[768]{0:T(1024)}, s32[768]{0:T(1024)S(1)}, u32[]{:S(2)}) copy-start(s32[768]{0:T(1024)S(1)} %get-tuple-element.101) | copy-start | bytes 9220
  38.0 7.6 copy-start.98
  44.8 16.8 %copy-start.17 = (f32[768,256]{0,1:T(8,128)}, f32[768,256]{0,1:T(8,128)S(1)}, u32[]{:S(2)}) copy-start(f32[768,256]{0,1:T(8,128)S(1)} %get-tuple-element.86) | copy-start | bytes 2359300
  44.8 5.9 copy-start.118
  44.8 10.8 %copy-start.74 = (bf16[320,256]{1,0:T(8,128)(2,1)S(1)}, bf16[320,256]{1,0:T(8,128)(2,1)}, u32[]{:S(2)}) copy-start(bf16[320,256]{1,0:T(8,128)(2,1)} %param.19) | copy-start | bytes 491524
  44.9 16.8 %copy-start.83 = (f32[768]{0:T(1024)}, f32[768]{0:T(1024)S(1)}, u32[]{:S(2)}) copy-start(f32[768]{0:T(1024)S(1)} %fusion.125) | copy-start | bytes 9220
  45.4 16.2 %copy-start.75 = (bf16[256,320]{0,1:T(8,128)(2,1)S(1)}, bf16[256,320]{0,1:T(8,128)(2,1)}, u32[]{:S(2)}) copy-start(bf16[256,320]{0,1:T(8,128)(2,1)} %param.24) | copy-start | bytes 491524
  47.2 23.0 %copy-start.31 = (bf16[768,128]{0,1:T(8,128)(2,1)}, bf16[768,128]{0,1:T(8,128)(2,1)S(1)}, u32[]{:S(2)}) copy-start(bf16[768,128]{0,1:T(8,128)(2,1)S(1)} %get-tuple-element.80) | copy-start | bytes 589828
  47.3 27.6 %collective-permute-start = (bf16[768,256]{0,1:T(8,128)(2,1)S(1)}, bf16[768,256]{0,1:T(8,128)(2,1)S(1)}, u32[]{:S(2)}, u32[]{:S(2)}) collective-permute-start(bf16[768,256]{0,1:T(8,128)(2,1)S(1)} %pad_maximum_fusion), channel_id=1, source_target_pairs={{0,4},{4,8},{8,12},{1,5},{5,9},{9,13},{2,6},{6,10},{10,14},{3,7},{... | collective-permute-start | bytes 1179656 | tf_op jit(solution)/shard_map/ppermute | solution.py:18
  55.0 13.5 %copy-start.100 = (f32[2,1,128]{2,1,0:T(1,128)}, f32[2,1,128]{2,1,0:T(1,128)S(1)}, u32[]{:S(2)}) copy-start(f32[2,1,128]{2,1,0:T(1,128)S(1)} %convert_element_type.259) | copy-start | bytes 3076
  61.6 6.9 copy-start.47
  67.6 39.3 %copy-start.27 = (bf16[256,640]{0,1:T(8,128)(2,1)}, bf16[256,640]{0,1:T(8,128)(2,1)S(1)}, u32[]{:S(2)}) copy-start(bf16[256,640]{0,1:T(8,128)(2,1)S(1)} %all_gather.45) | copy-start | bytes 983044
  70.2 31.6 %copy-start.68 = (bf16[768,128]{0,1:T(8,128)(2,1)}, bf16[768,128]{0,1:T(8,128)(2,1)S(1)}, u32[]{:S(2)}) copy-start(bf16[768,128]{0,1:T(8,128)(2,1)S(1)} %get-tuple-element.77) | copy-start | bytes 589828
  70.2 31.6 %copy-start.70 = (bf16[768,128]{0,1:T(8,128)(2,1)}, bf16[768,128]{0,1:T(8,128)(2,1)S(1)}, u32[]{:S(2)}) copy-start(bf16[768,128]{0,1:T(8,128)(2,1)S(1)} %get-tuple-element.78) | copy-start | bytes 589828
  71.0 32.7 %copy-start = (f32[1,768,768]{1,2,0:T(8,128)}, f32[1,768,768]{1,2,0:T(8,128)S(1)}, u32[]{:S(2)}) copy-start(f32[1,768,768]{1,2,0:T(8,128)S(1)} %get-tuple-element.96) | copy-start | bytes 7077892
  71.4 6.2 copy-start.42
  71.4 12.9 %collective-permute-start.4 = (bf16[768,256]{1,0:T(8,128)(2,1)S(1)}, bf16[768,256]{1,0:T(8,128)(2,1)S(1)}, u32[]{:S(2)}, u32[]{:S(2)}) collective-permute-start(bf16[768,256]{1,0:T(8,128)(2,1)S(1)} %collective-permute-done.3), channel_id=1, source_target_pairs={{0,4},{4,8},{8,12},{1,5},{5,9},{9,13},{2,6},{6,10},{10,14},{3,7},{... | collective-permute-start | bytes 1179656 | tf_op jit(solution)/shard_map/ppermute | solution.py:18
  74.9 17.2 %collective-permute-start.1 = (bf16[768,256]{0,1:T(8,128)(2,1)S(1)}, bf16[768,256]{0,1:T(8,128)(2,1)S(1)}, u32[]{:S(2)}, u32[]{:S(2)}) collective-permute-start(bf16[768,256]{0,1:T(8,128)(2,1)S(1)} %collective-permute-done), channel_id=1, source_target_pairs={{0,4},{4,8},{8,12},{1,5},{5,9},{9,13},{2,6},{6,10},{10,14},{3,7},{... | collective-permute-start | bytes 1179656 | tf_op jit(solution)/shard_map/ppermute | solution.py:18
  77.6 27.5 %copy-start.2 = (f32[1,768,768]{1,2,0:T(8,128)}, f32[1,768,768]{1,2,0:T(8,128)S(1)}, u32[]{:S(2)}) copy-start(f32[1,768,768]{1,2,0:T(8,128)S(1)} %get-tuple-element.94) | copy-start | bytes 7077892
  77.6 19.4 %copy-start.109 = (s32[768]{0:T(1024)S(1)}, s32[768]{0:T(1024)}, u32[]{:S(2)}) copy-start(s32[768]{0:T(1024)} %copy-done.108) | copy-start | bytes 9220
  77.7 19.4 %copy-start.113 = (s32[768]{0:T(1024)S(1)}, s32[768]{0:T(1024)}, u32[]{:S(2)}) copy-start(s32[768]{0:T(1024)} %copy-done.112) | copy-start | bytes 9220
  84.3 21.5 %copy-start.33 = (bf16[768,256]{1,0:T(8,128)(2,1)}, bf16[768,256]{1,0:T(8,128)(2,1)S(1)}, u32[]{:S(2)}) copy-start(bf16[768,256]{1,0:T(8,128)(2,1)S(1)} %collective-permute-done.4) | copy-start | bytes 1179652
  84.3 22.0 %collective-permute-start.5 = (bf16[768,256]{1,0:T(8,128)(2,1)S(1)}, bf16[768,256]{1,0:T(8,128)(2,1)S(1)}, u32[]{:S(2)}, u32[]{:S(2)}) collective-permute-start(bf16[768,256]{1,0:T(8,128)(2,1)S(1)} %collective-permute-done.4), channel_id=1, source_target_pairs={{0,4},{4,8},{8,12},{1,5},{5,9},{9,13},{2,6},{6,10},{10,14},{3,7},{... | collective-permute-start | bytes 1179656 | tf_op jit(solution)/shard_map/ppermute | solution.py:18
  92.1 5.6 copy-start.59
  92.1 9.7 %collective-permute-start.2 = (bf16[768,256]{0,1:T(8,128)(2,1)S(1)}, bf16[768,256]{0,1:T(8,128)(2,1)S(1)}, u32[]{:S(2)}, u32[]{:S(2)}) collective-permute-start(bf16[768,256]{0,1:T(8,128)(2,1)S(1)} %collective-permute-done.1), channel_id=1, source_target_pairs={{0,4},{4,8},{8,12},{1,5},{5,9},{9,13},{2,6},{6,10},{10,14},{3,7},{... | collective-permute-start | bytes 1179656 | tf_op jit(solution)/shard_map/ppermute | solution.py:18
  109.3 84.3 %all-reduce.23.cloned.1.call-start = ((), (), s32[]{:S(2)}) async-start(), calls=%async_computation.1 | async-start | bytes 1966080 | tf_op jit(solution)/shard_map/psum | solution.py:215
  109.3 18.6 %copy-start.67 = (bf16[512,320]{0,1:T(8,128)(2,1)S(1)}, bf16[512,320]{0,1:T(8,128)(2,1)}, u32[]{:S(2)}) copy-start(bf16[512,320]{0,1:T(8,128)(2,1)} %param.29) | copy-start | bytes 983044
  157.5 83.9 %all-reduce.25.cloned.1.call-start = ((), (), s32[]{:S(2)}) async-start(), calls=%async_computation.2 | async-start | bytes 1966080 | tf_op jit(solution)/shard_map/psum | solution.py:229
  193.6 4.9 copy-start.13
  193.6 4.9 copy-start.79
  205.4 161.8 %all-reduce.31.cloned.1.call-start = ((), (), s32[]{:S(2)}) async-start(), calls=%async_computation.5 | async-start | bytes 3538944 | tf_op jit(solution)/shard_map/psum | solution.py:292
  265.6 13.9 %collective-permute-start.9 = (bf16[768,256]{1,0:T(8,128)(2,1)S(1)}, bf16[768,256]{1,0:T(8,128)(2,1)S(1)}, u32[]{:S(2)}, u32[]{:S(2)}) collective-permute-start(bf16[768,256]{1,0:T(8,128)(2,1)S(1)} %convolution_convert_fusion.3), channel_id=1, source_target_pairs={{4,0},{8,4},{12,8},{5,1},{9,5},{13,9},{6,2},{10,6},{14,10},{7,3},{... | collective-permute-start | bytes 1179656 | tf_op jit(solution)/shard_map/ppermute | solution.py:18
  271.3 16.7 %collective-permute-start.6 = (bf16[768,256]{0,1:T(8,128)(2,1)S(1)}, bf16[768,256]{0,1:T(8,128)(2,1)S(1)}, u32[]{:S(2)}, u32[]{:S(2)}) collective-permute-start(bf16[768,256]{0,1:T(8,128)(2,1)S(1)} %fusion.53), channel_id=1, source_target_pairs={{4,0},{8,4},{12,8},{5,1},{9,5},{13,9},{6,2},{10,6},{14,10},{7,3},{... | collective-permute-start | bytes 1179656 | tf_op jit(solution)/shard_map/ppermute | solution.py:18
  280.1 16.3 %collective-permute-start.10 = (bf16[768,256]{1,0:T(8,128)(2,1)S(1)}, bf16[768,256]{1,0:T(8,128)(2,1)S(1)}, u32[]{:S(2)}, u32[]{:S(2)}) collective-permute-start(bf16[768,256]{1,0:T(8,128)(2,1)S(1)} %add_convert_fusion.3), channel_id=1, source_target_pairs={{4,0},{8,4},{12,8},{5,1},{9,5},{13,9},{6,2},{10,6},{14,10},{7,3},{... | collective-permute-start | bytes 1179656 | tf_op jit(solution)/shard_map/ppermute | solution.py:18
  288.5 16.3 %collective-permute-start.7 = (bf16[768,256]{0,1:T(8,128)(2,1)S(1)}, bf16[768,256]{0,1:T(8,128)(2,1)S(1)}, u32[]{:S(2)}, u32[]{:S(2)}) collective-permute-start(bf16[768,256]{0,1:T(8,128)(2,1)S(1)} %add_convert_fusion.6), channel_id=1, source_target_pairs={{4,0},{8,4},{12,8},{5,1},{9,5},{13,9},{6,2},{10,6},{14,10},{7,3},{... | collective-permute-start | bytes 1179656 | tf_op jit(solution)/shard_map/ppermute | solution.py:18
  290.0 16.2 %copy-start.48 = (bf16[640,256]{1,0:T(8,128)(2,1)S(1)}, bf16[640,256]{1,0:T(8,128)(2,1)}, u32[]{:S(2)}) copy-start(bf16[640,256]{1,0:T(8,128)(2,1)} %copy-done.47) | copy-start | bytes 983044
  296.5 16.8 %collective-permute-start.11 = (bf16[768,256]{1,0:T(8,128)(2,1)S(1)}, bf16[768,256]{1,0:T(8,128)(2,1)S(1)}, u32[]{:S(2)}, u32[]{:S(2)}) collective-permute-start(bf16[768,256]{1,0:T(8,128)(2,1)S(1)} %add_convert_fusion.2), channel_id=1, source_target_pairs={{4,0},{8,4},{12,8},{5,1},{9,5},{13,9},{6,2},{10,6},{14,10},{7,3},{... | collective-permute-start | bytes 1179656 | tf_op jit(solution)/shard_map/ppermute | solution.py:18
  304.9 14.8 %collective-permute-start.8 = (bf16[768,256]{0,1:T(8,128)(2,1)S(1)}, bf16[768,256]{0,1:T(8,128)(2,1)S(1)}, u32[]{:S(2)}, u32[]{:S(2)}) collective-permute-start(bf16[768,256]{0,1:T(8,128)(2,1)S(1)} %add_convert_fusion.5), channel_id=1, source_target_pairs={{4,0},{8,4},{12,8},{5,1},{9,5},{13,9},{6,2},{10,6},{14,10},{7,3},{... | collective-permute-start | bytes 1179656 | tf_op jit(solution)/shard_map/ppermute | solution.py:18
  314.1 6.5 copy-start.24
  320.6 286.4 %all-reduce.27.cloned.1.call-start = ((), (), s32[]{:S(2)}) async-start(), calls=%async_computation.3 | async-start | bytes 13107200 | tf_op jit(solution)/shard_map/psum | solution.py:12
  328.3 41.6 %copy-start.18 = (f32[768,256]{0,1:T(8,128)S(1)}, f32[768,256]{0,1:T(8,128)}, u32[]{:S(2)}) copy-start(f32[768,256]{0,1:T(8,128)} %copy-done.17) | copy-start | bytes 2359300
  328.3 41.6 %copy-start.84 = (f32[768]{0:T(1024)S(1)}, f32[768]{0:T(1024)}, u32[]{:S(2)}) copy-start(f32[768]{0:T(1024)} %copy-done.83) | copy-start | bytes 9220
  328.3 41.6 %copy-start.99 = (f32[2,1,128]{2,1,0:T(1,128)S(1)}, f32[2,1,128]{2,1,0:T(1,128)}, u32[]{:S(2)}) copy-start(f32[2,1,128]{2,1,0:T(1,128)} %copy-done.98) | copy-start | bytes 3076
  373.3 397.0 %all-reduce.29.cloned.1.call-start = ((), (), s32[]{:S(2)}) async-start(), calls=%async_computation.4 | async-start | bytes 13107200 | tf_op jit(solution)/shard_map/psum | solution.py:12
  607.0 7.0 copy-start.50
  607.0 7.5 copy-start.46
  614.6 33.0 %copy-start.92 = (f32[768]{0:T(1024)S(1)}, f32[768]{0:T(1024)}, u32[]{:S(2)}) copy-start(f32[768]{0:T(1024)} %copy-done.91) | copy-start | bytes 9220
  614.6 33.0 %copy-start.10 = (f32[768,640]{1,0:T(8,128)S(1)}, f32[768,640]{1,0:T(8,128)}, u32[]{:S(2)}) copy-start(f32[768,640]{1,0:T(8,128)} %copy-done.9) | copy-start | bytes 5898244
  770.3 5.4 copy-start.72
  770.3 6.2 copy-start.66
  770.3 7.0 copy-start.65
  (75 other events, 174.2 us)
Sparse Core Ops, SparseCore 0:
  109.4 35.7 all-reduce.20
  157.6 35.9 all-reduce.22
  205.5 35.8 all-reduce.24
  320.7 46.3 all-reduce.30
  373.4 233.5 all-reduce.26
  609.9 160.3 all-reduce.28
